TPU v7x, 32 devices: a whole 2x2x4 slice. The times are simulated.
32 devices in a mesh: fsdp: 2 (over x), ctx: 4 (over y, core), tp: 4 (over z).
Axes of the slice: x: 2, y: 2, z: 4, core: 2. Of those that a mesh axis runs over, the one named last changes fastest.
Arguments:
- tokens: bfloat16 [8, 512, 768], P(('fsdp', 'tp'), 'ctx'), may hold values from -6 to 6
- seg_ids: int32 [8, 512], P(('fsdp', 'tp')), may hold values from 0 to 2, never falling along the last dimension, each value on 1 to 384 neighbouring positions
- routes: int32 [8, 512, 2], P(('fsdp', 'tp'), 'ctx'), may hold values from 0 to 3, all different within a row; in each aligned block of 128 rows (0 to 127, 128 to 255, ..., all dimensions but the last counted through in order) at most 80 rows name the same one
- norm_attn: bfloat16 [768], P('fsdp'), may hold values from 0.5 to 1.5
- weight_qkv: bfloat16 [768, 2304], P('fsdp'), may hold values from -0.21875 to 0.21875
- weight_proj: bfloat16 [768, 768], P(None, 'fsdp'), may hold values from -0.875 to 0.875
- rel_table: float32 [12, 32], replicated, may hold values from -4 to 4
- norm_ffn: bfloat16 [768], P('fsdp'), may hold values from 0.5 to 1.5
- weight_router: bfloat16 [768, 4], P('fsdp'), may hold values from -0.21875 to 0.21875
- expert_up: bfloat16 [4, 768, 3072], P(None, 'fsdp', ('ctx', 'tp')), may hold values from -0.21875 to 0.21875
- expert_down: bfloat16 [4, 3072, 768], P(None, ('ctx', 'tp'), 'fsdp'), may hold values from -0.109375 to 0.109375
- cotangent: bfloat16 [8, 512, 768], P(('fsdp', 'tp'), 'ctx'), may hold values from -6 to 6
Outputs:
- output: bfloat16 [8, 512, 768], P(('fsdp', 'tp'), 'ctx')
- grad_tokens: float32 [8, 512, 768], P(('fsdp', 'tp'), 'ctx')
- grad_norm_attn: float32 [768], P('fsdp')
- grad_weight_qkv: float32 [768, 2304], P('fsdp')
- grad_weight_proj: float32 [768, 768], P(None, 'fsdp')
- grad_rel_table: float32 [12, 32], replicated
- grad_norm_ffn: float32 [768], P('fsdp')
- grad_weight_router: float32 [768, 4], P('fsdp')
- grad_expert_up: float32 [4, 768, 3072], P(None, 'fsdp', ('ctx', 'tp'))
- grad_expert_down: float32 [4, 3072, 768], P(None, ('ctx', 'tp'), 'fsdp')
Inputs may be any that keep to these rules, and one draw needn't show every extreme that they name: `seg_ids`: each group's 512 positions fall into at most 3 sequences whose numbers never fall along the positions; the longest has exactly 384 positions. `routes`: each token names two different experts. In each aligned block of 128 rows (the rows of one device) no expert is named more than 80 times, and in every draw some expert is named exactly 80 times in some block.
All inputs are finite; a program needn't handle non-finite values.
Results may differ from a plain program's by a relative error of at most 0.012.
Values may be sent and summed in bfloat16 or wider, within the bound.
A program may use at most 192 MiB of HBM per device.

v0:
```python
import jax
import jax.numpy as jnp
import numpy as np
from jax import lax
from jax.sharding import PartitionSpec as P

BUCKETS = 32
MAX_DISTANCE = 128
EPSILON = 1e-06
MASK_FILL = -1e30
F32 = jnp.float32
BF16 = jnp.bfloat16


def bucket_bounds(buckets, far_reach):
    exact_count = buckets // 2
    bounds = []
    for number in range(1, buckets):
        if number <= exact_count:
            bounds.append(number)
        else:
            exponent = (number - exact_count) / (buckets - exact_count)
            bounds.append(int(np.ceil(exact_count * (far_reach / exact_count) ** exponent)))
    return bounds


BOUNDS = bucket_bounds(BUCKETS, MAX_DISTANCE)


def rms_scale(values):
    return lax.rsqrt(jnp.mean(values * values, axis=-1, keepdims=True) + EPSILON)


def dot(a, b, ca, cb):
    return lax.dot_general(a, b, (((ca,), (cb,)), ((), ())), preferred_element_type=F32)


def exchange_sum(part, axis, dim):
    count = lax.axis_size(axis)
    size = part.shape[dim] // count
    me = lax.axis_index(axis)
    total = lax.dynamic_slice_in_dim(part, me * size, size, dim)
    for step in range(1, count):
        target = lax.rem(me + step, count)
        piece = lax.dynamic_slice_in_dim(part, target * size, size, dim).astype(BF16)
        total = total + lax.ppermute(
            piece, axis, [(i, (i + step) % count) for i in range(count)]
        ).astype(F32)
    return total


def local(
    tokens,
    seg_ids,
    routes,
    norm_attn,
    weight_qkv,
    weight_proj,
    rel_table,
    norm_ffn,
    weight_router,
    expert_up,
    expert_down,
    cotangent,
):
    rows = tokens.shape[1]
    width = tokens.shape[2]
    heads = rel_table.shape[0]
    head_size = width // heads
    ctx_count = lax.axis_size("ctx")
    heads_here = heads // ctx_count
    hw = heads_here * head_size
    experts = expert_up.shape[0]
    units = expert_up.shape[2]
    length = seg_ids.shape[1]
    score_scale = head_size ** (-0.5)
    ctx_index = lax.axis_index("ctx")
    fsdp_index = lax.axis_index("fsdp")
    own_width = norm_attn.shape[0]
    world = ("ctx", "tp")
    token_group = lax.all_gather(tokens[0], "ctx", axis=0, tiled=True)
    small = jnp.concatenate([norm_attn[None], norm_ffn[None], weight_router.T], axis=0)
    small = lax.all_gather(small, "fsdp", axis=1, tiled=True)
    gain_one = small[0].astype(F32)
    gain_two = small[1].astype(F32)
    router_t = small[2:]
    qkv_part = jnp.concatenate(
        [lax.dynamic_slice_in_dim(weight_qkv, s * width + ctx_index * hw, hw, 1) for s in range(3)],
        axis=1,
    )
    qkv_here = lax.all_gather(qkv_part, "fsdp", axis=0, tiled=True)
    proj_full = lax.all_gather(weight_proj, "fsdp", axis=1, tiled=True)
    route_all = lax.all_gather(routes[0], world, axis=0, tiled=True)
    up_t = lax.all_gather(
        jnp.swapaxes(expert_up, 1, 2).reshape(experts * units, own_width),
        "fsdp",
        axis=1,
        tiled=True,
    )
    down = lax.all_gather(
        expert_down.reshape(experts * units, own_width), "fsdp", axis=1, tiled=True
    )
    grad_all = lax.all_gather(cotangent[0], world, axis=0, tiled=True)
    block = MAX_DISTANCE
    table_here = lax.dynamic_slice_in_dim(rel_table, ctx_index * heads_here, heads_here, 0)
    offset = lax.broadcasted_iota(jnp.int32, (1, block, block), 1) - lax.broadcasted_iota(
        jnp.int32, (1, block, block), 2
    )

    def bias_block(distance):
        value = jnp.broadcast_to(table_here[:, 0][:, None, None], (heads_here, block, block))
        for number, bound in enumerate(BOUNDS, 1):
            value = jnp.where(distance >= bound, table_here[:, number][:, None, None], value)
        return value

    near = bias_block(offset)
    next_near = bias_block(offset + block)
    far = jnp.broadcast_to(table_here[:, BUCKETS - 1][:, None, None], (heads_here, block, block))
    blocks = length // block
    picks = {0: near, 1: next_near}
    bias = jnp.concatenate(
        [
            jnp.concatenate([picks.get(i - j, far) for j in range(blocks)], axis=2)
            for i in range(blocks)
        ],
        axis=1,
    )
    positions = jnp.arange(length, dtype=jnp.int32)
    segment = seg_ids[0]
    allowed = (segment[:, None] == segment[None, :]) & (positions[:, None] >= positions[None, :])
    bias = jnp.where(allowed[None], bias, MASK_FILL)
    inputs_group = token_group.astype(F32)
    normed_group = (inputs_group * rms_scale(inputs_group) * gain_one).astype(BF16)
    projected = dot(normed_group, qkv_here, 1, 0).astype(BF16)
    by_head = projected.reshape(length, 3, heads_here, head_size)
    query, key, value = (by_head[:, 0], by_head[:, 1], by_head[:, 2])
    scores = jnp.einsum("qhd,khd->hqk", query, key, preferred_element_type=F32) * score_scale + bias
    peak = jnp.max(scores, axis=-1, keepdims=True)
    weights = jnp.exp(scores - peak)
    probs = weights / jnp.sum(weights, axis=-1, keepdims=True)
    low_probs = probs.astype(BF16)
    attended = (
        jnp.einsum("hqk,khd->qhd", low_probs, value, preferred_element_type=F32)
        .astype(BF16)
        .reshape(length, hw)
    )
    mixed = lax.all_to_all(attended, "ctx", split_axis=0, concat_axis=1, tiled=True)
    inputs = tokens[0].astype(F32)
    scale_one = rms_scale(inputs)
    middle = inputs + dot(mixed, proj_full, 1, 0)
    scale_two = rms_scale(middle)
    normed_two = (middle * scale_two * gain_two).astype(BF16)
    normed_all = lax.all_gather(normed_two, world, axis=0, tiled=True)

    def gates_of(normed, route):
        logits = dot(normed, router_t, 1, 1)
        number = lax.broadcasted_iota(jnp.int32, (1, experts), 1)
        chosen = (route[:, 0:1] == number) | (route[:, 1:2] == number)
        masked = jnp.where(chosen, logits, MASK_FILL)
        raw = jnp.where(chosen, jnp.exp(masked - jnp.max(masked, axis=1, keepdims=True)), 0.0)
        return raw / jnp.sum(raw, axis=1, keepdims=True)

    gates_all = gates_of(normed_all, route_all)
    column = lax.broadcasted_iota(jnp.int32, (1, experts * units), 1) // units
    spread = gates_all[:, 0:1]
    for e in range(1, experts):
        spread = jnp.where(column >= e, gates_all[:, e : e + 1], spread)
    pre = dot(normed_all, up_t, 1, 1)
    reach = dot(grad_all, down, 1, 1)
    act, gelu_back = jax.vjp(jax.nn.gelu, pre)
    act = act.astype(BF16).astype(F32)
    gated = (act * spread).astype(BF16)
    product = act * reach
    dots_all = jnp.stack(
        [jnp.sum(jnp.where(column == e, product, 0.0), axis=1) for e in range(experts)], axis=0
    )
    grad_pre = gelu_back(reach * spread)[0].astype(BF16)
    total_rows = normed_all.shape[0]
    devices = total_rows // rows
    dots_all = jnp.swapaxes(dots_all.reshape(experts, devices, rows), 0, 1)
    dots_own = lax.psum_scatter(
        dots_all.reshape(devices, experts * rows), world, scatter_dimension=0, tiled=True
    )
    gate_dots = dots_own.reshape(experts, rows).T
    grad_normed_two = lax.psum_scatter(
        dot(grad_pre, up_t, 1, 0).astype(BF16), world, scatter_dimension=0, tiled=True
    ).astype(F32)
    result = lax.psum_scatter(
        dot(gated, down, 1, 0).astype(BF16), world, scatter_dimension=0, tiled=True
    ).astype(F32)
    output = (middle + result).astype(BF16)[None]
    grad_up = exchange_sum(dot(grad_pre, normed_all, 0, 0), "fsdp", 1)
    grad_up = jnp.swapaxes(grad_up.reshape(experts, units, own_width), 1, 2)
    grad_down = exchange_sum(dot(gated, grad_all, 0, 0), "fsdp", 1)
    grad_down = grad_down.reshape(experts, units, own_width)
    grad_out = cotangent[0].astype(F32)
    gates = gates_of(normed_two, routes[0])
    grad_logits = gates * (gate_dots - jnp.sum(gates * gate_dots, axis=1, keepdims=True))
    grad_normed_two = grad_normed_two + jnp.dot(
        grad_logits, router_t.astype(F32), precision=lax.Precision.HIGHEST
    )
    grad_router = lax.dot_general(
        grad_logits,
        normed_two.astype(F32),
        (((0,), (0,)), ((), ())),
        precision=lax.Precision.HIGHEST,
    )
    weighted_two = grad_normed_two * gain_two
    grad_gain_two = jnp.sum(grad_normed_two * middle * scale_two, axis=0)
    grad_middle = (
        grad_out
        + scale_two * weighted_two
        - middle * scale_two**3 * jnp.mean(weighted_two * middle, axis=1, keepdims=True)
    )
    grad_mid_group = lax.all_gather(grad_middle.astype(BF16), "ctx", axis=0, tiled=True)
    proj_rows = lax.dynamic_slice_in_dim(proj_full, ctx_index * hw, hw, 0)
    grad_attended = dot(grad_mid_group, proj_rows, 1, 1).astype(BF16)
    grad_heads = grad_attended.reshape(length, heads_here, head_size)
    grad_value = jnp.einsum("hqk,qhd->khd", low_probs, grad_heads, preferred_element_type=F32)
    grad_probs = jnp.einsum("qhd,khd->hqk", grad_heads, value, preferred_element_type=F32)
    grad_scores = (
        probs * (grad_probs - jnp.sum(probs * grad_probs, axis=-1, keepdims=True))
    ).astype(BF16)
    grad_query = (
        jnp.einsum("hqk,khd->qhd", grad_scores, key, preferred_element_type=F32) * score_scale
    )
    grad_key = (
        jnp.einsum("hqk,qhd->khd", grad_scores, query, preferred_element_type=F32) * score_scale
    )
    grad_qkv = jnp.concatenate(
        [
            grad_query.astype(BF16).reshape(length, hw),
            grad_key.astype(BF16).reshape(length, hw),
            grad_value.astype(BF16).reshape(length, hw),
        ],
        axis=1,
    )
    grad_normed_one = exchange_sum(dot(grad_qkv, qkv_here, 1, 1), "ctx", 0)
    weight_part = jnp.concatenate(
        [dot(normed_group, grad_qkv, 0, 0), dot(grad_mid_group, attended, 0, 0)], axis=1
    )
    weight_own = lax.psum_scatter(
        weight_part.astype(BF16), ("fsdp", "tp"), scatter_dimension=0, tiled=True
    )
    weight_all = lax.all_gather(weight_own, world, axis=0, tiled=True).astype(F32)
    weight_all = weight_all.reshape(ctx_count, own_width, 4 * hw)
    grad_weight_qkv = jnp.concatenate(
        [weight_all[c, :, s * hw : (s + 1) * hw] for s in range(3) for c in range(ctx_count)],
        axis=1,
    )
    grad_weight_proj = jnp.swapaxes(weight_all[:, :, 3 * hw :], 1, 2).reshape(width, own_width)

    def score_block(i, j):
        return grad_scores[:, i * block : (i + 1) * block, j * block : (j + 1) * block].astype(F32)

    near_sum = sum((score_block(i, i) for i in range(blocks)))
    next_sum = sum((score_block(i + 1, i) for i in range(blocks - 1)))
    far_sum = sum(
        (jnp.sum(score_block(i, j), axis=(1, 2)) for i in range(blocks) for j in range(i - 1))
    )
    lows = [0] + BOUNDS
    highs = BOUNDS + [2 * block]
    bucket_sums = [
        jnp.sum(jnp.where((offset >= lo) & (offset < hi), near_sum, 0.0), axis=(1, 2))
        + jnp.sum(
            jnp.where((offset + block >= lo) & (offset + block < hi), next_sum, 0.0), axis=(1, 2)
        )
        for lo, hi in zip(lows, highs)
    ]
    bucket_sums[-1] = bucket_sums[-1] + far_sum
    table_here_grad = jnp.stack(bucket_sums, axis=1)
    table_term = lax.dynamic_update_slice_in_dim(
        jnp.zeros((heads, BUCKETS), F32), table_here_grad, ctx_index * heads_here, 0
    )
    weighted_one = grad_normed_one * gain_one
    grad_gain_one = jnp.sum(grad_normed_one * inputs * scale_one, axis=0)
    grad_tokens = (
        grad_middle
        + scale_one * weighted_one
        - inputs * scale_one**3 * jnp.mean(weighted_one * inputs, axis=1, keepdims=True)
    )
    packed = jnp.concatenate(
        [grad_gain_one, grad_gain_two, grad_router.reshape(-1), table_term.reshape(-1)]
    ).reshape(-1, 128)
    packed = lax.psum(packed, ("fsdp", "ctx", "tp")).reshape(-1)
    gains = packed[: (2 + experts) * width].reshape(2 + experts, width)
    gains = lax.dynamic_slice_in_dim(gains, fsdp_index * own_width, own_width, 1)
    table_grad = packed[(2 + experts) * width :].reshape(heads, BUCKETS)
    return (
        output,
        grad_tokens[None],
        gains[0],
        grad_weight_qkv,
        grad_weight_proj,
        table_grad,
        gains[1],
        gains[2:].T,
        grad_up,
        grad_down,
    )


def solution(mesh):
    rows = P(("fsdp", "tp"), "ctx", None)
    in_specs = (
        rows,
        P(("fsdp", "tp"), None),
        rows,
        P("fsdp"),
        P("fsdp", None),
        P(None, "fsdp"),
        P(),
        P("fsdp"),
        P("fsdp", None),
        P(None, "fsdp", ("ctx", "tp")),
        P(None, ("ctx", "tp"), "fsdp"),
        rows,
    )
    out_specs = (
        rows,
        rows,
        P("fsdp"),
        P("fsdp", None),
        P(None, "fsdp"),
        P(),
        P("fsdp"),
        P("fsdp", None),
        P(None, "fsdp", ("ctx", "tp")),
        P(None, ("ctx", "tp"), "fsdp"),
    )
    return jax.shard_map(local, mesh=mesh, in_specs=in_specs, out_specs=out_specs, check_vma=False)
```

profile of v0, /device:TPU:0, one launch (start us, length us, event | category | flops | bytes accessed | tf_op | source)
XLA Modules:
  0.0 534.5 jit_solution(10073200459211450725)
XLA Ops:
  11.4 20.5 %all_gather.35 = bf16[768,576]{1,0:T(8,128)(2,1)S(1)} all-gather(bf16[384,576]{1,0:T(8,128)(2,1)S(1)} %pad_maximum_fusion.2), channel_id=1, replica_groups=mesh['fsdp'=2,'ctx'=4,'tp'=4] {'fsdp'}, dimensions={0}, use_global_device_ids=true | all-gather | bytes 1327104 | tf_op jit(solution)/shard_map/all_gather | solution.py:91
  32.0 4.9 all_gather.34
  37.6 8.4 %all-gather = bf16[1,512,768]{2,1,0:T(8,128)(2,1)S(1)} all-gather(bf16[1,128,768]{2,1,0:T(8,128)(2,1)S(1)} %copy-done.6), channel_id=2, replica_groups=mesh['fsdp'=2,'ctx'=4,'tp'=4] {'ctx'}, dimensions={1}, use_global_device_ids=true | all-gather | bytes 983040 | tf_op jit(solution)/shard_map/all_gather | solution.py:81
  51.6 4.9 convolution_convert_fusion.6
  56.7 8.4 %all_to_all.19 = bf16[4,128,192]{1,2,0:T(8,128)(2,1)} all-to-all(bf16[4,128,192]{1,2,0:T(8,128)(2,1)S(1)} %copy.59), channel_id=1, replica_groups=mesh['fsdp'=2,'ctx'=4,'tp'=4] {'ctx'}, dimensions={0} | all-to-all | bytes 393216 | tf_op jit(solution)/shard_map/all_to_all | solution.py:147
  70.2 31.9 %all-gather.1 = s32[1,2048,2]{1,2,0:T(2,128)S(1)} all-gather(s32[1,128,2]{1,2,0:T(2,128)S(1)} %copy-done.68), channel_id=3, replica_groups=mesh['fsdp'=2,'ctx'=4,'tp'=4] {'ctx','tp'}, dimensions={1}, use_global_device_ids=true | all-gather | bytes 17408 | tf_op jit(solution)/shard_map/all_gather | solution.py:93
  104.5 10.3 %all-gather.12.cloned.1.call-done = bf16[2048,768]{1,0:T(8,128)(2,1)} async-done(((bf16[128,768]{1,0:T(8,128)(2,1)}), bf16[2048,768]{1,0:T(8,128)(2,1)}) %all-gather.12.cloned.1.call-update) | async-done | bytes 3145744 | tf_op jit(solution)/shard_map/all_gather | solution.py:153
  114.9 2.8 fusion.257
  118.4 19.6 %all-gather.14.cloned.1.call-done = bf16[768,768]{1,0:T(8,128)(2,1)} async-done(((bf16[768,384]{1,0:T(8,128)(2,1)}), bf16[768,768]{1,0:T(8,128)(2,1)}) %all-gather.14.cloned.1.call-update) | async-done | bytes 1179664 | tf_op jit(solution)/shard_map/all_gather | solution.py:94
  138.0 7.5 %fusion.259 = f32[2048,768]{0,1:T(8,128)} fusion(bf16[2048,768]{1,0:T(8,128)(2,1)} %all-gather.12.cloned.1.call-done, bf16[768,768]{1,0:T(8,128)(2,1)} %all-gather.14.cloned.1.call-done), kind=kOutput, calls=%fused_computation.499 | convolution fusion | flops 2415919104 | bytes 10616832 | tf_op jit(solution)/shard_map/dot_general | solution.py:35
  145.5 16.7 %all-gather.16.cloned.1.call-done = bf16[768,768]{1,0:T(8,128)(2,1)} async-done(((bf16[768,384]{1,0:T(8,128)(2,1)}), bf16[768,768]{1,0:T(8,128)(2,1)}) %all-gather.16.cloned.1.call-update) | async-done | bytes 1179664 | tf_op jit(solution)/shard_map/all_gather | solution.py:100
  162.2 47.4 %all-gather.20.cloned.1.call-done = bf16[1,2048,768]{2,1,0:T(8,128)(2,1)} async-done(((bf16[1,128,768]{2,1,0:T(8,128)(2,1)}), bf16[1,2048,768]{2,1,0:T(8,128)(2,1)}) %all-gather.20.cloned.1.call-update) | async-done | bytes 3145744 | tf_op jit(solution)/shard_map/all_gather | solution.py:103
  209.6 15.3 %select_reduce_fusion.3 = (f32[2048]{0:T(1024)}, f32[2048]{0:T(1024)}, f32[2048]{0:T(1024)}, f32[2048]{0:T(1024)}, bf16[2048,768]{0,1:T(8,128)(2,1)}, /*index=5*/bf16[2048,768]{0,1:T(8,128)(2,1)S(1)}) fusion(pred[768]{0:T(1024)(128)(4,1)} %get-tuple-element.174, pred[768]{0:T(1024)(128)(4,1)} %get-tuple-element.175, pred[768]{0:T(1024)(128)(4,1)} %get-tuple-element.170, ...), kind=kOutput, calls=%fused_computation.16 | convolution fusion | flops 2472534016 | bytes 16979200 | tf_op jit(solution)/shard_map/dot_general | solution.py:35
  226.6 4.1 convolution_convert_fusion
  249.5 7.5 %convolution_convert_fusion.1 = bf16[2048,768]{1,0:T(8,128)(2,1)} fusion(bf16[768,768]{1,0:T(8,128)(2,1)} %all-gather.16.cloned.1.call-done, bf16[2048,768]{0,1:T(8,128)(2,1)} %get-tuple-element.126, f32[2048]{0:T(1024)S(1)} %bitcast.258, f32[2048]{0:T(1024)} %bitcast.261, f32[2048]{0:T(1024)} %bitcast.264, f32[2048]{0:T(1024)S(1)} %bitcast.255, ...), kind=kOutput, calls=%fused_computation.20 | convolution fusion | flops 2426929152 | bytes 7506176 | tf_op jit(solution)/shard_map/dot_general | solution.py:35
  263.2 6.3 %fusion.10 = f32[768,768]{1,0:T(8,128)S(1)} fusion(bf16[1,2048,768]{2,1,0:T(8,128)(2,1)} %all-gather.20.cloned.1.call-done, bf16[2048,768]{0,1:T(8,128)(2,1)} %get-tuple-element.126, f32[2048]{0:T(1024)} %bitcast.259, f32[2048]{0:T(1024)} %bitcast.262, f32[2048]{0:T(1024)} %bitcast.265, f32[2048]{0:T(1024)} %bitcast.256, ...), kind=kOutput, calls=%fused_computation.23 | convolution fusion | flops 2425356288 | bytes 8685824 | tf_op jit(solution)/shard_map/dot_general | solution.py:35
  272.0 2.6 fusion.260
  277.5 60.8 %all-reduce = f32[16,512]{1,0:T(8,128)} all-reduce(f32[16,512]{1,0:T(8,128)} %bitcast.247), channel_id=7, replica_groups=mesh['fsdp'=2,'ctx'=4,'tp'=4] {'ctx','tp'}, use_global_device_ids=true, to_apply=%region_14.15.clone | all-reduce | flops 8192 | bytes 65536
  343.9 2.7 convert_add_fusion
  346.7 2.2 convert_add_fusion.1
  348.9 2.8 multiply_reduce_fusion.1
  351.7 13.4 %reduce-scatter.6.cloned.1.call-done = bf16[128,768]{1,0:T(8,128)(2,1)} async-done(((bf16[2048,768]{1,0:T(8,128)(2,1)}), bf16[128,768]{1,0:T(8,128)(2,1)}) %reduce-scatter.6.cloned.1.call-update) | async-done | bytes 196624 | tf_op jit(solution)/shard_map/reduce_scatter | solution.py:188
  365.1 2.3 fusion.252
  367.3 8.1 %all_gather.42 = bf16[512,768]{1,0:T(8,128)(2,1)S(1)} all-gather(bf16[128,768]{1,0:T(8,128)(2,1)S(1)} %get-tuple-element.124), channel_id=1, replica_groups=mesh['fsdp'=2,'ctx'=4,'tp'=4] {'ctx'}, dimensions={0}, use_global_device_ids=true | all-gather | bytes 983040 | tf_op jit(solution)/shard_map/all_gather | solution.py:215
  379.1 2.7 multiply_convert_fusion.1
  384.2 4.5 convolution_convert_fusion.5
  395.5 2.1 select_reduce_fusion.5
  413.5 42.9 %reduce-scatter.10.cloned.1.call-done = bf16[96,768]{1,0:T(8,128)(2,1)} async-done(((bf16[768,768]{1,0:T(8,128)(2,1)}), bf16[96,768]{1,0:T(8,128)(2,1)}) %reduce-scatter.10.cloned.1.call-update) | async-done | bytes 147472 | tf_op jit(solution)/shard_map/reduce_scatter | solution.py:242
  464.2 3.2 collective-permute-done
  469.0 3.9 collective-permute-done.2
  474.1 40.1 %psum.7 = f32[39,128]{1,0:T(8,128)S(1)} all-reduce(f32[39,128]{1,0:T(8,128)S(1)} %maximum_bitcast_fusion), channel_id=1, replica_groups=mesh['fsdp'=2,'ctx'=4,'tp'=4] {'fsdp','ctx','tp'}, use_global_device_ids=true, to_apply=%region_89.90 | all-reduce | flops 4992 | bytes 39936 | tf_op jit(solution)/shard_map/psum | solution.py:285
  523.1 4.7 concatenate.45
  (392 shorter events, 103.6 us)
Async XLA Ops:
  7.2 24.8 %copy-start.73 = (bf16[384]{0:T(512)(128)(2,1)S(1)}, bf16[384]{0:T(512)(128)(2,1)}, u32[]{:S(2)}) copy-start(bf16[384]{0:T(512)(128)(2,1)} %param.15) | copy-start | bytes 2308
  7.2 24.8 %copy-start.74 = (bf16[384]{0:T(512)(128)(2,1)S(1)}, bf16[384]{0:T(512)(128)(2,1)}, u32[]{:S(2)}) copy-start(bf16[384]{0:T(512)(128)(2,1)} %param.19) | copy-start | bytes 2308
  7.2 24.8 %copy-start.70 = (bf16[384,4]{0,1:T(4,128)(2,1)S(1)}, bf16[384,4]{0,1:T(4,128)(2,1)}, u32[]{:S(2)}) copy-start(bf16[384,4]{0,1:T(4,128)(2,1)} %param.20) | copy-start | bytes 9220
  7.2 30.3 %copy-start.6 = (bf16[1,128,768]{2,1,0:T(8,128)(2,1)S(1)}, bf16[1,128,768]{2,1,0:T(8,128)(2,1)}, u32[]{:S(2)}) copy-start(bf16[1,128,768]{2,1,0:T(8,128)(2,1)} %param.12) | copy-start | bytes 589828
  7.2 57.8 %all-gather.10.cloned.1.call-start = ((), (), s32[]{:S(2)}) async-start(), calls=%async_computation.4 | async-start | bytes 1769472 | tf_op jit(solution)/shard_map/all_gather | solution.py:92
  8.0 106.9 %all-gather.12.cloned.1.call-start = ((), (), s32[]{:S(2)}) async-start(), calls=%async_computation.5 | async-start | bytes 3342336 | tf_op jit(solution)/shard_map/all_gather | solution.py:153
  9.2 37.1 %copy-start.59 = (s32[1,512]{1,0:T(1,128)S(1)}, s32[1,512]{1,0:T(1,128)}, u32[]{:S(2)}) copy-start(s32[1,512]{1,0:T(1,128)} %param.13) | copy-start | bytes 6148
  37.6 29.9 %copy-start.25 = (f32[768]{0:T(1024)}, f32[768]{0:T(1024)S(1)}, u32[]{:S(2)}) copy-start(f32[768]{0:T(1024)S(1)} %get-tuple-element.87) | copy-start | bytes 9220
  51.6 326.1 %copy-start.2 = (f32[3,512,512]{1,2,0:T(8,128)}, f32[3,512,512]{1,2,0:T(8,128)S(1)}, u32[]{:S(2)}) copy-start(f32[3,512,512]{1,2,0:T(8,128)S(1)} %get-tuple-element.160) | copy-start | bytes 9437188
  67.4 37.1 %copy-start.67 = (f32[128]{0:T(128)}, f32[128]{0:T(128)S(1)}, u32[]{:S(2)}) copy-start(f32[128]{0:T(128)S(1)} %get-tuple-element.158) | copy-start | bytes 1540
  68.2 69.8 %all-gather.14.cloned.1.call-start = ((), (), s32[]{:S(2)}) async-start(), calls=%async_computation.6 | async-start | bytes 1769472 | tf_op jit(solution)/shard_map/all_gather | solution.py:94
  69.0 93.3 %all-gather.16.cloned.1.call-start = ((), (), s32[]{:S(2)}) async-start(), calls=%async_computation.7 | async-start | bytes 1769472 | tf_op jit(solution)/shard_map/all_gather | solution.py:100
  69.6 140.1 %all-gather.20.cloned.1.call-start = ((), (), s32[]{:S(2)}) async-start(), calls=%async_computation.11 | async-start | bytes 3342336 | tf_op jit(solution)/shard_map/all_gather | solution.py:103
  70.1 278.7 %reduce-scatter.8.cloned.1.call-start = ((), (), s32[]{:S(2)}) async-start(), calls=%async_computation.9 | async-start | bytes 3342336 | tf_op jit(solution)/shard_map/reduce_scatter | solution.py:185
  118.4 131.1 %copy-start.60 = (f32[2048,1]{0,1:T(1,128)}, f32[2048,1]{0,1:T(1,128)S(1)}, u32[]{:S(2)}) copy-start(f32[2048,1]{0,1:T(1,128)S(1)} %get-tuple-element.147) | copy-start | bytes 24580
  118.4 131.1 %copy-start.61 = (f32[2048,1]{0,1:T(1,128)}, f32[2048,1]{0,1:T(1,128)S(1)}, u32[]{:S(2)}) copy-start(f32[2048,1]{0,1:T(1,128)S(1)} %get-tuple-element.148) | copy-start | bytes 24580
  230.7 134.4 %reduce-scatter.6.cloned.1.call-start = ((), (), s32[]{:S(2)}) async-start(), calls=%async_computation.8 | async-start | bytes 3342336 | tf_op jit(solution)/shard_map/reduce_scatter | solution.py:188
  257.0 199.4 %reduce-scatter.10.cloned.1.call-start = ((), (), s32[]{:S(2)}) async-start(), calls=%async_computation.12 | async-start | bytes 1327104 | tf_op jit(solution)/shard_map/reduce_scatter | solution.py:242
  270.5 73.4 %collective-permute-start.4 = (bf16[768,384]{1,0:T(8,128)(2,1)}, bf16[768,384]{1,0:T(8,128)(2,1)}, u32[]{:S(2)}, u32[]{:S(2)}) collective-permute-start(bf16[768,384]{1,0:T(8,128)(2,1)} %dynamic-slice_convert_fusion), channel_id=1, source_target_pairs={{0,16},{16,0},{1,17},{17,1},{2,18},{18,2},{3,19},{19,3},{4,20},{20... | collective-permute-start | bytes 1769480 | tf_op jit(solution)/shard_map/ppermute | solution.py:46
  276.3 70.4 %collective-permute-start.3 = (bf16[768,384]{1,0:T(8,128)(2,1)}, bf16[768,384]{1,0:T(8,128)(2,1)}, u32[]{:S(2)}, u32[]{:S(2)}) collective-permute-start(bf16[768,384]{1,0:T(8,128)(2,1)} %dynamic-slice_convert_fusion.1), channel_id=1, source_target_pairs={{0,16},{16,0},{1,17},{17,1},{2,18},{18,2},{3,19},{19,3},{4,20},{20... | collective-permute-start | bytes 1769480 | tf_op jit(solution)/shard_map/ppermute | solution.py:46
  276.9 72.0 %copy-start.26 = (f32[768]{0:T(1024)S(1)}, f32[768]{0:T(1024)}, u32[]{:S(2)}) copy-start(f32[768]{0:T(1024)} %copy-done.25) | copy-start | bytes 9220
  391.4 66.3 %copy-start.23 = (bf16[3,64,512]{2,1,0:T(8,128)(2,1)S(1)}, bf16[3,64,512]{2,1,0:T(8,128)(2,1)}, u32[]{:S(2)}) copy-start(bf16[3,64,512]{2,1,0:T(8,128)(2,1)} %fusion.17) | copy-start | bytes 589828
  391.4 66.3 %copy-start.24 = (bf16[3,64,512]{2,1,0:T(8,128)(2,1)S(1)}, bf16[3,64,512]{2,1,0:T(8,128)(2,1)}, u32[]{:S(2)}) copy-start(bf16[3,64,512]{2,1,0:T(8,128)(2,1)} %fusion.18) | copy-start | bytes 589828
  392.9 64.9 %copy-start.16 = (bf16[768,576]{1,0:T(8,128)(2,1)S(1)}, bf16[768,576]{1,0:T(8,128)(2,1)}, u32[]{:S(2)}) copy-start(bf16[768,576]{1,0:T(8,128)(2,1)} %copy-done.15) | copy-start | bytes 2654212
  392.9 124.3 %all-gather.18.cloned.1.call-start = ((), (), s32[]{:S(2)}) async-start(), calls=%async_computation.10 | async-start | bytes 2506752 | tf_op jit(solution)/shard_map/all_gather | solution.py:245
  397.7 75.2 %copy-start.7 = (bf16[1,128,768]{2,1,0:T(8,128)(2,1)S(1)}, bf16[1,128,768]{2,1,0:T(8,128)(2,1)}, u32[]{:S(2)}) copy-start(bf16[1,128,768]{2,1,0:T(8,128)(2,1)} %param.12) | copy-start | bytes 589828
  397.7 75.2 %copy-start.71 = (f32[128]{0:T(128)S(1)}, f32[128]{0:T(128)}, u32[]{:S(2)}) copy-start(f32[128]{0:T(128)} %get-tuple-element.156) | copy-start | bytes 1540
  457.8 58.5 %copy-start.11 = (f32[128,768]{1,0:T(8,128)S(1)}, f32[128,768]{1,0:T(8,128)}, u32[]{:S(2)}) copy-start(f32[128,768]{1,0:T(8,128)} %get-tuple-element.125) | copy-start | bytes 1179652
  457.8 58.5 %copy-start.75 = (f32[128]{0:T(128)S(1)}, f32[128]{0:T(128)}, u32[]{:S(2)}) copy-start(f32[128]{0:T(128)} %get-tuple-element.155) | copy-start | bytes 1540
  460.8 6.6 %collective-permute-start = (bf16[128,768]{1,0:T(8,128)(2,1)S(1)}, bf16[128,768]{1,0:T(8,128)(2,1)S(1)}, u32[]{:S(2)}, u32[]{:S(2)}) collective-permute-start(bf16[128,768]{1,0:T(8,128)(2,1)S(1)} %get-tuple-element.143), channel_id=1, source_target_pairs={{0,4},{4,8},{8,12},{12,0},{1,5},{5,9},{9,13},{13,1},{2,6},{6,10},{... | collective-permute-start | bytes 589832 | tf_op jit(solution)/shard_map/ppermute | solution.py:46
  460.9 8.1 %collective-permute-start.1 = (bf16[128,768]{1,0:T(8,128)(2,1)S(1)}, bf16[128,768]{1,0:T(8,128)(2,1)S(1)}, u32[]{:S(2)}, u32[]{:S(2)}) collective-permute-start(bf16[128,768]{1,0:T(8,128)(2,1)S(1)} %get-tuple-element.145), channel_id=1, source_target_pairs={{0,8},{4,12},{8,0},{12,4},{1,9},{5,13},{9,1},{13,5},{2,10},{6,14},... | collective-permute-start | bytes 589832 | tf_op jit(solution)/shard_map/ppermute | solution.py:46
  462.4 10.4 %collective-permute-start.2 = (bf16[128,768]{1,0:T(8,128)(2,1)S(1)}, bf16[128,768]{1,0:T(8,128)(2,1)S(1)}, u32[]{:S(2)}, u32[]{:S(2)}) collective-permute-start(bf16[128,768]{1,0:T(8,128)(2,1)S(1)} %get-tuple-element.144), channel_id=1, source_target_pairs={{0,12},{4,0},{8,4},{12,8},{1,13},{5,1},{9,5},{13,9},{2,14},{6,2},{... | collective-permute-start | bytes 589832 | tf_op jit(solution)/shard_map/ppermute | solution.py:46
  (61 other events, 305.5 us)
Sparse Core Ops, SparseCore 0:
  9.6 29.6 all-gather.9
  68.4 46.4 all-gather.11
  116.4 21.5 all-gather.13
  139.4 22.7 all-gather.15
  164.4 45.1 all-gather.19
  230.8 65.1 reduce-scatter.7
  299.8 65.2 reduce-scatter.5
  393.0 63.3 reduce-scatter.9
  458.7 42.8 all-gather.17
where the time goes:
time: 542 us; the launch traced here: 535 us
  blocking collectives  183 us (34%)
  waiting for transfers between devices  161 us (30%)
  matrix products  73.5 us (14%)
  other arithmetic  64.2 us (12%)
  local copies, waits for them, and re-layouts  31 us (6%)
  between operations  15.5 us (3%)
  starting transfers between devices  5.8 us (1%)
    unnamed x1, blocking collectives  60.8 us
    dot_general x14, matrix products, dot(): lax.dot_general(a, b, (((ca,), (cb,)), ((), ())), preferred_element_type=...  55.1 us
    all_gather x1, waiting for transfers between devices, local(): grad_all = lax.all_gather(cotangent[0], world, axis=0, tiled=True)  47.4 us
    reduce_scatter x1, waiting for transfers between devices, local(): lax.psum_scatter(weight_part.astype(BF16), ('fsdp', 'tp'), scatter_dimens...  42.9 us
    psum x1, blocking collectives, local(): packed = lax.psum(packed, ('fsdp', 'ctx', 'tp')).reshape(-1)  40.1 us
    all_gather x1, blocking collectives, local(): route_all = lax.all_gather(routes[0], world, axis=0, tiled=True)  31.9 us
    all_gather x1, blocking collectives, local(): qkv_here = lax.all_gather(qkv_part, 'fsdp', axis=0, tiled=True)  20.5 us
    all_gather x1, waiting for transfers between devices, local(): lax.all_gather(jnp.swapaxes(expert_up, 1, 2).reshape(experts * units, own...  19.6 us
  transfers between devices with their start and end apart: 14, of which 9 were waited for; matrix products, arithmetic and copies ran while one was open for 21% of the time, Pallas kernels for 0%

commit v1 on v0

--- a/solution.py
+++ b/solution.py
@@ -282,7 +282,7 @@
     packed = jnp.concatenate(
         [grad_gain_one, grad_gain_two, grad_router.reshape(-1), table_term.reshape(-1)]
     ).reshape(-1, 128)
-    packed = lax.psum(packed, ("fsdp", "ctx", "tp")).reshape(-1)
+    packed = jnp.sum(lax.all_gather(packed, ("fsdp", "ctx", "tp")), axis=0).reshape(-1)
     gains = packed[: (2 + experts) * width].reshape(2 + experts, width)
     gains = lax.dynamic_slice_in_dim(gains, fsdp_index * own_width, own_width, 1)
     table_grad = packed[(2 + experts) * width :].reshape(heads, BUCKETS)

time: 542 us -> 577 us (1.065)
  blocking collectives: 183 us -> 217 us
  waiting for transfers between devices: 161 us -> 176 us
  other arithmetic: 64.2 us -> 50.9 us
    all_gather x0 -> x1, blocking collectives: none -> 74.3 us  [local(): lax.all_gather(packed, ('fsdp', 'ctx', 'tp'))]
    psum x1 -> x0, blocking collectives: 40.1 us -> none  [local(): packed = lax.psum(packed, ('fsdp', 'ctx', 'tp')).reshape(-1)]
    reduce_scatter x1, waiting for transfers between devices: 42.9 us -> 57.7 us  [local(): lax.psum_scatter(weight_part.astype(BF16), ('fsdp', 'tp'), scatter_dimens...]
    add x31, other arithmetic: 11.4 us -> 0.12 us  [local(): jnp.sum(jnp.where((offset >= lo) & (offset < hi), near_sum, 0.0), axis=(1...]
  transfers between devices with their start and end apart: 14 -> 14, of which waited for: 9 -> 9; matrix products, arithmetic and copies ran while one was open for 21% -> 17% of each run, Pallas kernels for 0% -> 0%
where the time goes in v1:
time: 577 us; the launch traced here: 571 us
  blocking collectives  217 us (38%)
  waiting for transfers between devices  176 us (31%)
  matrix products  73.5 us (13%)
  other arithmetic  50.9 us (9%)
  local copies, waits for them, and re-layouts  31 us (5%)
  between operations  15.8 us (3%)
  starting transfers between devices  6.07 us (1%)
    all_gather x1, blocking collectives, local(): lax.all_gather(packed, ('fsdp', 'ctx', 'tp'))  74.3 us
    unnamed x1, blocking collectives  60.6 us
    reduce_scatter x1, waiting for transfers between devices, local(): lax.psum_scatter(weight_part.astype(BF16), ('fsdp', 'tp'), scatter_dimens...  57.7 us
    dot_general x14, matrix products, dot(): lax.dot_general(a, b, (((ca,), (cb,)), ((), ())), preferred_element_type=...  55 us
    all_gather x1, waiting for transfers between devices, local(): grad_all = lax.all_gather(cotangent[0], world, axis=0, tiled=True)  47.4 us
    all_gather x1, blocking collectives, local(): route_all = lax.all_gather(routes[0], world, axis=0, tiled=True)  31.8 us
    all_gather x1, blocking collectives, local(): qkv_here = lax.all_gather(qkv_part, 'fsdp', axis=0, tiled=True)  20.5 us
    all_gather x1, waiting for transfers between devices, local(): lax.all_gather(jnp.swapaxes(expert_up, 1, 2).reshape(experts * units, own...  19.6 us
  transfers between devices with their start and end apart: 14, of which 9 were waited for; matrix products, arithmetic and copies ran while one was open for 17% of the time, Pallas kernels for 0%

profile of v1, /device:TPU:0, one launch (start us, length us, event | category | flops | bytes accessed | tf_op | source)
XLA Modules:
  0.0 570.5 jit_solution(11758089445244145037)
XLA Ops:
  11.4 20.5 %all_gather.38 = bf16[768,576]{1,0:T(8,128)(2,1)S(1)} all-gather(bf16[384,576]{1,0:T(8,128)(2,1)S(1)} %pad_maximum_fusion.2), channel_id=1, replica_groups=mesh['fsdp'=2,'ctx'=4,'tp'=4] {'fsdp'}, dimensions={0}, use_global_device_ids=true | all-gather | bytes 1327104 | tf_op jit(solution)/shard_map/all_gather | solution.py:91
  32.0 4.9 all_gather.37
  37.6 8.4 %all-gather = bf16[1,512,768]{2,1,0:T(8,128)(2,1)S(1)} all-gather(bf16[1,128,768]{2,1,0:T(8,128)(2,1)S(1)} %copy-done.6), channel_id=2, replica_groups=mesh['fsdp'=2,'ctx'=4,'tp'=4] {'ctx'}, dimensions={1}, use_global_device_ids=true | all-gather | bytes 983040 | tf_op jit(solution)/shard_map/all_gather | solution.py:81
  51.6 4.9 convolution_convert_fusion.6
  56.7 8.4 %all_to_all.19 = bf16[4,128,192]{1,2,0:T(8,128)(2,1)} all-to-all(bf16[4,128,192]{1,2,0:T(8,128)(2,1)S(1)} %copy.59), channel_id=1, replica_groups=mesh['fsdp'=2,'ctx'=4,'tp'=4] {'ctx'}, dimensions={0} | all-to-all | bytes 393216 | tf_op jit(solution)/shard_map/all_to_all | solution.py:147
  70.2 31.8 %all-gather.1 = s32[1,2048,2]{1,2,0:T(2,128)S(1)} all-gather(s32[1,128,2]{1,2,0:T(2,128)S(1)} %copy-done.80), channel_id=3, replica_groups=mesh['fsdp'=2,'ctx'=4,'tp'=4] {'ctx','tp'}, dimensions={1}, use_global_device_ids=true | all-gather | bytes 17408 | tf_op jit(solution)/shard_map/all_gather | solution.py:93
  104.4 10.5 %all-gather.12.cloned.1.call-done = bf16[2048,768]{1,0:T(8,128)(2,1)} async-done(((bf16[128,768]{1,0:T(8,128)(2,1)}), bf16[2048,768]{1,0:T(8,128)(2,1)}) %all-gather.12.cloned.1.call-update) | async-done | bytes 3145744 | tf_op jit(solution)/shard_map/all_gather | solution.py:153
  114.9 2.8 fusion.257
  118.5 19.6 %all-gather.14.cloned.1.call-done = bf16[768,768]{1,0:T(8,128)(2,1)} async-done(((bf16[768,384]{1,0:T(8,128)(2,1)}), bf16[768,768]{1,0:T(8,128)(2,1)}) %all-gather.14.cloned.1.call-update) | async-done | bytes 1179664 | tf_op jit(solution)/shard_map/all_gather | solution.py:94
  138.1 7.5 %fusion.259 = f32[2048,768]{0,1:T(8,128)} fusion(bf16[2048,768]{1,0:T(8,128)(2,1)} %all-gather.12.cloned.1.call-done, bf16[768,768]{1,0:T(8,128)(2,1)} %all-gather.14.cloned.1.call-done), kind=kOutput, calls=%fused_computation.499 | convolution fusion | flops 2415919104 | bytes 10616832 | tf_op jit(solution)/shard_map/dot_general | solution.py:35
  145.6 16.7 %all-gather.16.cloned.1.call-done = bf16[768,768]{1,0:T(8,128)(2,1)} async-done(((bf16[768,384]{1,0:T(8,128)(2,1)}), bf16[768,768]{1,0:T(8,128)(2,1)}) %all-gather.16.cloned.1.call-update) | async-done | bytes 1179664 | tf_op jit(solution)/shard_map/all_gather | solution.py:100
  162.3 47.4 %all-gather.20.cloned.1.call-done = bf16[1,2048,768]{2,1,0:T(8,128)(2,1)} async-done(((bf16[1,128,768]{2,1,0:T(8,128)(2,1)}), bf16[1,2048,768]{2,1,0:T(8,128)(2,1)}) %all-gather.20.cloned.1.call-update) | async-done | bytes 3145744 | tf_op jit(solution)/shard_map/all_gather | solution.py:103
  209.7 15.3 %select_reduce_fusion.3 = (f32[2048]{0:T(1024)}, f32[2048]{0:T(1024)}, f32[2048]{0:T(1024)}, f32[2048]{0:T(1024)}, bf16[2048,768]{0,1:T(8,128)(2,1)}, /*index=5*/bf16[2048,768]{0,1:T(8,128)(2,1)S(1)}) fusion(pred[768]{0:T(1024)(128)(4,1)} %get-tuple-element.174, pred[768]{0:T(1024)(128)(4,1)} %get-tuple-element.175, pred[768]{0:T(1024)(128)(4,1)} %get-tuple-element.170, ...), kind=kOutput, calls=%fused_computation.16 | convolution fusion | flops 2472534016 | bytes 16979200 | tf_op jit(solution)/shard_map/dot_general | solution.py:35
  226.7 4.1 convolution_convert_fusion
  249.6 7.5 %convolution_convert_fusion.1 = bf16[2048,768]{1,0:T(8,128)(2,1)} fusion(bf16[768,768]{1,0:T(8,128)(2,1)} %all-gather.16.cloned.1.call-done, bf16[2048,768]{0,1:T(8,128)(2,1)} %get-tuple-element.126, f32[2048]{0:T(1024)S(1)} %bitcast.258, f32[2048]{0:T(1024)} %bitcast.261, f32[2048]{0:T(1024)} %bitcast.264, f32[2048]{0:T(1024)S(1)} %bitcast.255, ...), kind=kOutput, calls=%fused_computation.20 | convolution fusion | flops 2426929152 | bytes 7506176 | tf_op jit(solution)/shard_map/dot_general | solution.py:35
  263.6 6.3 %fusion.10 = f32[768,768]{1,0:T(8,128)S(1)} fusion(bf16[1,2048,768]{2,1,0:T(8,128)(2,1)} %all-gather.20.cloned.1.call-done, bf16[2048,768]{0,1:T(8,128)(2,1)} %get-tuple-element.126, f32[2048]{0:T(1024)} %bitcast.259, f32[2048]{0:T(1024)} %bitcast.262, f32[2048]{0:T(1024)} %bitcast.265, f32[2048]{0:T(1024)} %bitcast.256, ...), kind=kOutput, calls=%fused_computation.23 | convolution fusion | flops 2425356288 | bytes 8685824 | tf_op jit(solution)/shard_map/dot_general | solution.py:35
  272.4 2.6 fusion.260
  277.9 60.6 %all-reduce = f32[16,512]{1,0:T(8,128)} all-reduce(f32[16,512]{1,0:T(8,128)} %bitcast.247), channel_id=7, replica_groups=mesh['fsdp'=2,'ctx'=4,'tp'=4] {'ctx','tp'}, use_global_device_ids=true, to_apply=%region_14.15.clone | all-reduce | flops 8192 | bytes 65536
  344.1 2.7 convert_add_fusion
  346.8 2.2 convert_add_fusion.1
  349.1 2.8 multiply_reduce_fusion.1
  351.8 13.3 %reduce-scatter.6.cloned.1.call-done = bf16[128,768]{1,0:T(8,128)(2,1)} async-done(((bf16[2048,768]{1,0:T(8,128)(2,1)}), bf16[128,768]{1,0:T(8,128)(2,1)}) %reduce-scatter.6.cloned.1.call-update) | async-done | bytes 196624 | tf_op jit(solution)/shard_map/reduce_scatter | solution.py:188
  365.1 2.3 fusion.252
  367.4 8.1 %all_gather.45 = bf16[512,768]{1,0:T(8,128)(2,1)S(1)} all-gather(bf16[128,768]{1,0:T(8,128)(2,1)S(1)} %get-tuple-element.124), channel_id=1, replica_groups=mesh['fsdp'=2,'ctx'=4,'tp'=4] {'ctx'}, dimensions={0}, use_global_device_ids=true | all-gather | bytes 983040 | tf_op jit(solution)/shard_map/all_gather | solution.py:215
  379.2 2.7 multiply_convert_fusion.1
  384.2 4.5 convolution_convert_fusion.5
  398.8 57.7 %reduce-scatter.10.cloned.1.call-done = bf16[96,768]{1,0:T(8,128)(2,1)} async-done(((bf16[768,768]{1,0:T(8,128)(2,1)}), bf16[96,768]{1,0:T(8,128)(2,1)}) %reduce-scatter.10.cloned.1.call-update) | async-done | bytes 147472 | tf_op jit(solution)/shard_map/reduce_scatter | solution.py:242
  466.0 3.9 collective-permute-done
  469.8 2.1 collective-permute-done.1
  472.0 2.6 collective-permute-done.2
  475.8 74.3 %all_gather.46 = f32[32,39,128]{2,1,0:T(8,128)S(1)} all-gather(f32[1,39,128]{2,1,0:T(8,128)S(1)} %maximum_bitcast_fusion), channel_id=1, replica_groups=mesh['fsdp'=2,'ctx'=4,'tp'=4] {'fsdp','ctx','tp'}, dimensions={0}, use_global_device_ids=true | all-gather | bytes 658944 | tf_op jit(solution)/shard_map/all_gather | solution.py:285
  559.1 4.7 concatenate.45
  (419 shorter events, 91.1 us)
Async XLA Ops:
  7.2 24.8 %copy-start.86 = (bf16[384]{0:T(512)(128)(2,1)S(1)}, bf16[384]{0:T(512)(128)(2,1)}, u32[]{:S(2)}) copy-start(bf16[384]{0:T(512)(128)(2,1)} %param.15) | copy-start | bytes 2308
  7.2 24.8 %copy-start.87 = (bf16[384]{0:T(512)(128)(2,1)S(1)}, bf16[384]{0:T(512)(128)(2,1)}, u32[]{:S(2)}) copy-start(bf16[384]{0:T(512)(128)(2,1)} %param.19) | copy-start | bytes 2308
  7.2 24.8 %copy-start.82 = (bf16[384,4]{0,1:T(4,128)(2,1)S(1)}, bf16[384,4]{0,1:T(4,128)(2,1)}, u32[]{:S(2)}) copy-start(bf16[384,4]{0,1:T(4,128)(2,1)} %param.20) | copy-start | bytes 9220
  7.2 30.3 %copy-start.6 = (bf16[1,128,768]{2,1,0:T(8,128)(2,1)S(1)}, bf16[1,128,768]{2,1,0:T(8,128)(2,1)}, u32[]{:S(2)}) copy-start(bf16[1,128,768]{2,1,0:T(8,128)(2,1)} %param.12) | copy-start | bytes 589828
  7.2 57.8 %all-gather.10.cloned.1.call-start = ((), (), s32[]{:S(2)}) async-start(), calls=%async_computation.4 | async-start | bytes 1769472 | tf_op jit(solution)/shard_map/all_gather | solution.py:92
  8.0 107.0 %all-gather.12.cloned.1.call-start = ((), (), s32[]{:S(2)}) async-start(), calls=%async_computation.5 | async-start | bytes 3342336 | tf_op jit(solution)/shard_map/all_gather | solution.py:153
  9.2 37.1 %copy-start.71 = (s32[1,512]{1,0:T(1,128)S(1)}, s32[1,512]{1,0:T(1,128)}, u32[]{:S(2)}) copy-start(s32[1,512]{1,0:T(1,128)} %param.13) | copy-start | bytes 6148
  37.6 29.9 %copy-start.25 = (f32[768]{0:T(1024)}, f32[768]{0:T(1024)S(1)}, u32[]{:S(2)}) copy-start(f32[768]{0:T(1024)S(1)} %get-tuple-element.87) | copy-start | bytes 9220
  51.6 326.1 %copy-start.2 = (f32[3,512,512]{1,2,0:T(8,128)}, f32[3,512,512]{1,2,0:T(8,128)S(1)}, u32[]{:S(2)}) copy-start(f32[3,512,512]{1,2,0:T(8,128)S(1)} %get-tuple-element.160) | copy-start | bytes 9437188
  67.4 37.0 %copy-start.79 = (f32[128]{0:T(128)}, f32[128]{0:T(128)S(1)}, u32[]{:S(2)}) copy-start(f32[128]{0:T(128)S(1)} %get-tuple-element.158) | copy-start | bytes 1540
  68.3 69.9 %all-gather.14.cloned.1.call-start = ((), (), s32[]{:S(2)}) async-start(), calls=%async_computation.6 | async-start | bytes 1769472 | tf_op jit(solution)/shard_map/all_gather | solution.py:94
  69.0 93.3 %all-gather.16.cloned.1.call-start = ((), (), s32[]{:S(2)}) async-start(), calls=%async_computation.7 | async-start | bytes 1769472 | tf_op jit(solution)/shard_map/all_gather | solution.py:100
  69.6 140.1 %all-gather.20.cloned.1.call-start = ((), (), s32[]{:S(2)}) async-start(), calls=%async_computation.11 | async-start | bytes 3342336 | tf_op jit(solution)/shard_map/all_gather | solution.py:103
  70.2 278.9 %reduce-scatter.8.cloned.1.call-start = ((), (), s32[]{:S(2)}) async-start(), calls=%async_computation.9 | async-start | bytes 3342336 | tf_op jit(solution)/shard_map/reduce_scatter | solution.py:185
  118.5 131.1 %copy-start.72 = (f32[2048,1]{0,1:T(1,128)}, f32[2048,1]{0,1:T(1,128)S(1)}, u32[]{:S(2)}) copy-start(f32[2048,1]{0,1:T(1,128)S(1)} %get-tuple-element.147) | copy-start | bytes 24580
  118.5 131.1 %copy-start.73 = (f32[2048,1]{0,1:T(1,128)}, f32[2048,1]{0,1:T(1,128)S(1)}, u32[]{:S(2)}) copy-start(f32[2048,1]{0,1:T(1,128)S(1)} %get-tuple-element.148) | copy-start | bytes 24580
  230.8 134.4 %reduce-scatter.6.cloned.1.call-start = ((), (), s32[]{:S(2)}) async-start(), calls=%async_computation.8 | async-start | bytes 3342336 | tf_op jit(solution)/shard_map/reduce_scatter | solution.py:188
  257.1 199.4 %reduce-scatter.10.cloned.1.call-start = ((), (), s32[]{:S(2)}) async-start(), calls=%async_computation.12 | async-start | bytes 1327104 | tf_op jit(solution)/shard_map/reduce_scatter | solution.py:242
  270.9 73.3 %collective-permute-start.4 = (bf16[768,384]{1,0:T(8,128)(2,1)}, bf16[768,384]{1,0:T(8,128)(2,1)}, u32[]{:S(2)}, u32[]{:S(2)}) collective-permute-start(bf16[768,384]{1,0:T(8,128)(2,1)} %dynamic-slice_convert_fusion), channel_id=1, source_target_pairs={{0,16},{16,0},{1,17},{17,1},{2,18},{18,2},{3,19},{19,3},{4,20},{20... | collective-permute-start | bytes 1769480 | tf_op jit(solution)/shard_map/ppermute | solution.py:46
  276.7 70.1 %collective-permute-start.3 = (bf16[768,384]{1,0:T(8,128)(2,1)}, bf16[768,384]{1,0:T(8,128)(2,1)}, u32[]{:S(2)}, u32[]{:S(2)}) collective-permute-start(bf16[768,384]{1,0:T(8,128)(2,1)} %dynamic-slice_convert_fusion.1), channel_id=1, source_target_pairs={{0,16},{16,0},{1,17},{17,1},{2,18},{18,2},{3,19},{19,3},{4,20},{20... | collective-permute-start | bytes 1769480 | tf_op jit(solution)/shard_map/ppermute | solution.py:46
  277.3 71.8 %copy-start.26 = (f32[768]{0:T(1024)S(1)}, f32[768]{0:T(1024)}, u32[]{:S(2)}) copy-start(f32[768]{0:T(1024)} %copy-done.25) | copy-start | bytes 9220
  391.3 68.1 %copy-start.23 = (bf16[3,64,512]{2,1,0:T(8,128)(2,1)S(1)}, bf16[3,64,512]{2,1,0:T(8,128)(2,1)}, u32[]{:S(2)}) copy-start(bf16[3,64,512]{2,1,0:T(8,128)(2,1)} %fusion.17) | copy-start | bytes 589828
  391.4 68.1 %copy-start.24 = (bf16[3,64,512]{2,1,0:T(8,128)(2,1)S(1)}, bf16[3,64,512]{2,1,0:T(8,128)(2,1)}, u32[]{:S(2)}) copy-start(bf16[3,64,512]{2,1,0:T(8,128)(2,1)} %fusion.18) | copy-start | bytes 589828
  392.9 66.6 %copy-start.16 = (bf16[768,576]{1,0:T(8,128)(2,1)S(1)}, bf16[768,576]{1,0:T(8,128)(2,1)}, u32[]{:S(2)}) copy-start(bf16[768,576]{1,0:T(8,128)(2,1)} %copy-done.15) | copy-start | bytes 2654212
  392.9 160.2 %all-gather.18.cloned.1.call-start = ((), (), s32[]{:S(2)}) async-start(), calls=%async_computation.10 | async-start | bytes 2506752 | tf_op jit(solution)/shard_map/all_gather | solution.py:245
  395.8 78.8 %copy-start.7 = (bf16[1,128,768]{2,1,0:T(8,128)(2,1)S(1)}, bf16[1,128,768]{2,1,0:T(8,128)(2,1)}, u32[]{:S(2)}) copy-start(bf16[1,128,768]{2,1,0:T(8,128)(2,1)} %param.12) | copy-start | bytes 589828
  395.8 78.8 %copy-start.83 = (f32[128]{0:T(128)S(1)}, f32[128]{0:T(128)}, u32[]{:S(2)}) copy-start(f32[128]{0:T(128)} %get-tuple-element.156) | copy-start | bytes 1540
  459.5 92.8 %copy-start.11 = (f32[128,768]{1,0:T(8,128)S(1)}, f32[128,768]{1,0:T(8,128)}, u32[]{:S(2)}) copy-start(f32[128,768]{1,0:T(8,128)} %get-tuple-element.125) | copy-start | bytes 1179652
  459.5 92.8 %copy-start.88 = (f32[128]{0:T(128)S(1)}, f32[128]{0:T(128)}, u32[]{:S(2)}) copy-start(f32[128]{0:T(128)} %get-tuple-element.155) | copy-start | bytes 1540
  462.5 7.3 %collective-permute-start = (bf16[128,768]{1,0:T(8,128)(2,1)S(1)}, bf16[128,768]{1,0:T(8,128)(2,1)S(1)}, u32[]{:S(2)}, u32[]{:S(2)}) collective-permute-start(bf16[128,768]{1,0:T(8,128)(2,1)S(1)} %get-tuple-element.143), channel_id=1, source_target_pairs={{0,4},{4,8},{8,12},{12,0},{1,5},{5,9},{9,13},{13,1},{2,6},{6,10},{... | collective-permute-start | bytes 589832 | tf_op jit(solution)/shard_map/ppermute | solution.py:46
  462.6 9.4 %collective-permute-start.1 = (bf16[128,768]{1,0:T(8,128)(2,1)S(1)}, bf16[128,768]{1,0:T(8,128)(2,1)S(1)}, u32[]{:S(2)}, u32[]{:S(2)}) collective-permute-start(bf16[128,768]{1,0:T(8,128)(2,1)S(1)} %get-tuple-element.145), channel_id=1, source_target_pairs={{0,8},{4,12},{8,0},{12,4},{1,9},{5,13},{9,1},{13,5},{2,10},{6,14},... | collective-permute-start | bytes 589832 | tf_op jit(solution)/shard_map/ppermute | solution.py:46
  464.1 10.4 %collective-permute-start.2 = (bf16[128,768]{1,0:T(8,128)(2,1)S(1)}, bf16[128,768]{1,0:T(8,128)(2,1)S(1)}, u32[]{:S(2)}, u32[]{:S(2)}) collective-permute-start(bf16[128,768]{1,0:T(8,128)(2,1)S(1)} %get-tuple-element.144), channel_id=1, source_target_pairs={{0,12},{4,0},{8,4},{12,8},{1,13},{5,1},{9,5},{13,9},{2,14},{6,2},{... | collective-permute-start | bytes 589832 | tf_op jit(solution)/shard_map/ppermute | solution.py:46
  (74 other events, 367.4 us)
Sparse Core Ops, SparseCore 0:
  9.6 29.6 all-gather.9
  68.4 46.5 all-gather.11
  116.5 21.5 all-gather.13
  139.5 22.7 all-gather.15
  164.5 45.1 all-gather.19
  230.9 65.0 reduce-scatter.7
  299.8 65.2 reduce-scatter.5
  393.1 63.3 reduce-scatter.9
  458.8 42.7 all-gather.17
